TPU v7x, 32 devices: a whole 2x2x4 slice. The times are simulated.
32 devices in a mesh: grp: 4 (over y, x), tp: 8 (over z, core).
Axes of the slice: x: 2, y: 2, z: 4, core: 2. Of those that a mesh axis runs over, the one named last changes fastest.
Arguments:
- layer_input: bfloat16 [8192, 2048], P('grp'), may hold values from -6 to 6
- out_cotangent: bfloat16 [8192, 2048], P('grp'), may hold values from -6 to 6
- seq_group: int32 [6], replicated, may hold values from 0 to 3, as said below
- seq_len: int32 [6], replicated, may hold values from 512 to 2048, as said below
- w_qkv: float32 [2048, 6144], P('grp', 'tp'), may hold values from -0.1875 to 0.1875
- b_qv: float32 [4096], replicated, may hold values from -3 to 3
- w_out: float32 [2048, 2048], P('grp', 'tp'), may hold values from -0.75 to 0.75
- b_out: float32 [2048], replicated, may hold values from -2 to 2
- w_up: float32 [2048, 8192], P('grp', 'tp'), may hold values from -0.125 to 0.125
- b_up: float32 [8192], replicated, may hold values from -3 to 3
- w_down: float32 [2048, 8192], P('grp', 'tp'), may hold values from -0.0625 to 0.0625
- b_down: float32 [2048], replicated, may hold values from -2 to 2
- first_norm_gain: float32 [2048], replicated, may hold values from 0.1 to 1.9
- first_norm_bias: float32 [2048], replicated, may hold values from -2 to 2
- second_norm_gain: float32 [2048], replicated, may hold values from 0.1 to 1.9
- second_norm_bias: float32 [2048], replicated, may hold values from -2 to 2
Outputs:
- layer_output: bfloat16 [8192, 2048], P(('grp', 'tp'))
- grad_x: float32 [8192, 2048], P(('grp', 'tp'))
- grad_w_qkv: float32 [2048, 6144], P('grp', 'tp')
- grad_b_qv: float32 [4096], replicated
- grad_w_out: float32 [2048, 2048], P('grp', 'tp')
- grad_b_out: float32 [2048], replicated
- grad_w_up: float32 [2048, 8192], P('grp', 'tp')
- grad_b_up: float32 [8192], replicated
- grad_w_down: float32 [2048, 8192], P('grp', 'tp')
- grad_b_down: float32 [2048], replicated
- grad_ln1_gain: float32 [2048], replicated
- grad_ln1_bias: float32 [2048], replicated
- grad_ln2_gain: float32 [2048], replicated
- grad_ln2_bias: float32 [2048], replicated
Inputs may be any that keep to these rules, and one draw needn't show every extreme that they name: `seq_group`: each group's sequences total at most 2048 tokens, and in every draw some group holds exactly 2048; every group holds at least one sequence. `seq_len`: each sequence has 2048 or 512 tokens.
All inputs are finite; a program needn't handle non-finite values.
Results may differ from a plain program's by a relative error of at most 0.023.
Values may be sent and summed in bfloat16 or wider, within the bound.
A program may use at most 320 MiB of HBM per device.

v0:
```python
import jax
import jax.numpy as jnp
from jax import lax
from jax.sharding import PartitionSpec as P

HD = 128


def layer_normalize(rows, gain, bias):
    mean_row = jnp.mean(rows, -1, keepdims=True)
    centred = rows - mean_row
    inverse = lax.rsqrt(jnp.mean(centred * centred, -1, keepdims=True) + 1e-05)
    normed = centred * inverse
    return (normed * gain + bias, normed, inverse)


def norm_backward_pass(grad_norm, normed, inverse, gain):
    scaled = grad_norm * gain
    inner = jnp.mean(scaled, -1, keepdims=True) + normed * jnp.mean(
        scaled * normed, -1, keepdims=True
    )
    return inverse * (scaled - inner)


def contract(left, right, left_dim, right_dim):
    return lax.dot_general(
        left, right, (((left_dim,), (right_dim,)), ((), ())), preferred_element_type=jnp.float32
    )


def activate(values_in):
    return jax.nn.gelu(values_in, approximate=True)


def on_device(
    layer_input,
    out_cotangent,
    seq_group,
    seq_len,
    w_qkv,
    b_qv,
    w_out,
    b_out,
    w_up,
    b_up,
    w_down,
    b_down,
    first_norm_gain,
    first_norm_bias,
    second_norm_gain,
    second_norm_bias,
):
    w_attn, w_proj, w_expand, w_reduce = (
        lax.all_gather(w_qkv.astype(jnp.bfloat16), "grp", axis=0, tiled=True),
        lax.all_gather(w_out.astype(jnp.bfloat16), "grp", axis=0, tiled=True),
        lax.all_gather(w_up.astype(jnp.bfloat16), "grp", axis=0, tiled=True),
        lax.all_gather(w_down.astype(jnp.bfloat16), "grp", axis=0, tiled=True),
    )
    tp_rank = lax.axis_index("tp")
    tp_count = lax.axis_size("tp")
    group_rank = lax.axis_index("grp")
    length = layer_input.shape[0]
    shared_row_block = length // tp_count
    local_row_start = tp_rank * shared_row_block
    heads_here = w_proj.shape[1] // HD
    hidden_here = w_expand.shape[1]
    seq_count = seq_group.shape[0]
    in_group = seq_group == group_rank
    lengths = jnp.where(in_group, seq_len, 0)
    seq_order = jnp.arange(seq_count, dtype=jnp.int32)
    earlier = seq_order[:, None] > seq_order[None, :]
    offsets = jnp.sum(jnp.where(earlier, lengths[None, :], 0), 1)
    places = jnp.arange(length, dtype=jnp.int32)
    inside = (
        in_group[None, :]
        & (places[:, None] >= offsets[None, :])
        & (places[:, None] < (offsets + lengths)[None, :])
    )
    segment = jnp.sum(jnp.where(inside, seq_order[None, :] + 1, 0), 1) - 1
    live_rows = (segment >= 0).astype(jnp.float32)[:, None]
    input_row_block = layer_input.astype(jnp.float32)
    first_normalized, first_standardized, first_inverse_deviation = layer_normalize(
        input_row_block, first_norm_gain, first_norm_bias
    )
    normed_oneb = first_normalized.astype(jnp.bfloat16)
    head_bias = lax.dynamic_slice_in_dim(
        b_qv.reshape(-1, 2, HD), tp_rank * heads_here, heads_here, 0
    )
    bias_three = jnp.stack(
        [head_bias[:, 0], jnp.zeros_like(head_bias[:, 0]), head_bias[:, 1]], 1
    ).reshape(-1)
    projected = (
        jnp.dot(normed_oneb, w_attn, preferred_element_type=jnp.float32) + bias_three
    ).astype(jnp.bfloat16)
    projected = projected.reshape(length, heads_here, 3, HD)
    query = projected[:, :, 0]
    keys = projected[:, :, 1]
    values = projected[:, :, 2]
    block_rows = min(512, length)
    blocks = length // block_rows
    score_scale = HD ** (-0.5)
    columns = jnp.arange(length, dtype=jnp.int32)

    def scores_for(block_index):
        first_row = block_index * block_rows
        query_block = lax.dynamic_slice_in_dim(query, first_row, block_rows, 0)
        dotted = (
            jnp.einsum("qhe,khe->hqk", query_block, keys, preferred_element_type=jnp.float32)
            * score_scale
        )
        segment_block = lax.dynamic_slice_in_dim(segment, first_row, block_rows, 0)
        row_places = first_row + jnp.arange(block_rows, dtype=jnp.int32)
        allowed = (segment_block[:, None] == segment[None, :]) & (
            columns[None, :] <= row_places[:, None]
        )
        return (jnp.where(allowed[None], dotted, -1e30), query_block)

    def attend(block_index):
        masked, unused = scores_for(block_index)
        highest_score = jnp.max(masked, -1, keepdims=True)
        powers = jnp.exp(masked - highest_score)
        summed = jnp.sum(powers, -1, keepdims=True)
        chances = (powers / summed).astype(jnp.bfloat16)
        context = jnp.einsum(
            "hqk,khe->qhe", chances, values, preferred_element_type=jnp.float32
        ).astype(jnp.bfloat16)
        return (context, highest_score[..., 0] + jnp.log(summed[..., 0]))

    contexts, log_totals = lax.map(attend, jnp.arange(blocks))
    context_all = contexts.reshape(length, heads_here * HD)
    attn_total = lax.psum(contract(context_all, w_proj, 1, 1).astype(jnp.bfloat16), "tp").astype(
        jnp.float32
    )
    hidden_input = input_row_block + attn_total + b_out
    second_normalized, second_standardized, second_inverse_deviation = layer_normalize(
        hidden_input, second_norm_gain, second_norm_bias
    )
    normed_twob = second_normalized.astype(jnp.bfloat16)
    up_bias = lax.dynamic_slice_in_dim(b_up, tp_rank * hidden_here, hidden_here, 0)
    before = jnp.dot(normed_twob, w_expand, preferred_element_type=jnp.float32) + up_bias
    active = activate(before).astype(jnp.bfloat16)
    live_share = lax.dynamic_slice_in_dim(live_rows, local_row_start, shared_row_block, 0)
    mlp_total = lax.psum(contract(active, w_reduce, 1, 1).astype(jnp.bfloat16), "tp").astype(
        jnp.float32
    )
    out_share = (
        lax.dynamic_slice_in_dim(hidden_input, local_row_start, shared_row_block, 0)
        + lax.dynamic_slice_in_dim(mlp_total, local_row_start, shared_row_block, 0)
        + b_down
    )
    result = (live_share * out_share).astype(jnp.bfloat16)
    output_gradient = out_cotangent.astype(jnp.float32) * live_rows
    grad_outb = output_gradient.astype(jnp.bfloat16)
    grad_share = lax.dynamic_slice_in_dim(output_gradient, local_row_start, shared_row_block, 0)
    grad_reduce = contract(grad_outb, active, 0, 0)
    grad_active = jnp.dot(grad_outb, w_reduce, preferred_element_type=jnp.float32)
    unused, gelu_back = jax.vjp(activate, before)
    grad_beforeb = gelu_back(grad_active)[0].astype(jnp.bfloat16)
    grad_expand = contract(normed_twob, grad_beforeb, 0, 0)
    up_bias_part = jnp.sum(grad_beforeb.astype(jnp.float32), 0)
    second_norm_gradient = lax.psum(
        contract(grad_beforeb, w_expand, 1, 1).astype(jnp.bfloat16), "tp"
    ).astype(jnp.float32)
    hidden_gradient = output_gradient + norm_backward_pass(
        second_norm_gradient, second_standardized, second_inverse_deviation, second_norm_gain
    )
    grad_resb = hidden_gradient.astype(jnp.bfloat16)
    residual_share_gradient = lax.dynamic_slice_in_dim(
        hidden_gradient, local_row_start, shared_row_block, 0
    )
    second_norm_shared = lax.dynamic_slice_in_dim(
        second_norm_gradient, local_row_start, shared_row_block, 0
    )
    gain_two_grad = jnp.sum(
        second_norm_shared
        * lax.dynamic_slice_in_dim(second_standardized, local_row_start, shared_row_block, 0),
        0,
    )
    bias_two_grad = jnp.sum(second_norm_shared, 0)
    bias_out_grad = jnp.sum(residual_share_gradient, 0)
    down_bias_grad = jnp.sum(grad_share, 0)
    grad_proj = contract(grad_resb, context_all, 0, 0)
    grad_context = (
        jnp.dot(grad_resb, w_proj, preferred_element_type=jnp.float32)
        .astype(jnp.bfloat16)
        .reshape(length, heads_here, HD)
    )

    def attend_back(running, block_index):
        grad_keys, grad_values = running
        masked, query_block = scores_for(block_index)
        chances = jnp.exp(masked - log_totals[block_index][..., None])
        grad_block = lax.dynamic_slice_in_dim(grad_context, block_index * block_rows, block_rows, 0)
        grad_values = grad_values + jnp.einsum(
            "hqk,qhe->khe",
            chances.astype(jnp.bfloat16),
            grad_block,
            preferred_element_type=jnp.float32,
        )
        grad_chances = jnp.einsum(
            "qhe,khe->hqk", grad_block, values, preferred_element_type=jnp.float32
        )
        grad_scores = (
            chances * (grad_chances - jnp.sum(chances * grad_chances, -1, keepdims=True))
        ).astype(jnp.bfloat16)
        grad_query = (
            jnp.einsum("hqk,khe->qhe", grad_scores, keys, preferred_element_type=jnp.float32)
            * score_scale
        )
        grad_keys = (
            grad_keys
            + jnp.einsum(
                "hqk,qhe->khe", grad_scores, query_block, preferred_element_type=jnp.float32
            )
            * score_scale
        )
        return ((grad_keys, grad_values), grad_query)

    zeros_heads = jnp.zeros((length, heads_here, HD), jnp.float32)
    (grad_keys, grad_values), grad_queries = lax.scan(
        attend_back, (zeros_heads, zeros_heads), jnp.arange(blocks)
    )
    grad_queries = grad_queries.reshape(length, heads_here, HD)
    grad_projected = (
        jnp.stack([grad_queries, grad_keys, grad_values], 2)
        .astype(jnp.bfloat16)
        .reshape(length, heads_here * 3 * HD)
    )
    grad_attn = contract(normed_oneb, grad_projected, 0, 0)
    projected_sums = jnp.sum(grad_projected.astype(jnp.float32), 0).reshape(heads_here, 3, HD)
    query_value = jnp.stack([projected_sums[:, 0], projected_sums[:, 2]], 1)
    query_value_full = lax.dynamic_update_slice_in_dim(
        jnp.zeros((b_qv.shape[0] // (2 * HD), 2, HD), jnp.float32),
        query_value,
        tp_rank * heads_here,
        0,
    ).reshape(-1)
    up_bias_full = lax.dynamic_update_slice_in_dim(
        jnp.zeros(b_up.shape, jnp.float32), up_bias_part, tp_rank * hidden_here, 0
    )
    first_norm_gradient = lax.dynamic_slice_in_dim(
        lax.psum(contract(grad_projected, w_attn, 1, 1).astype(jnp.bfloat16), "tp").astype(
            jnp.float32
        ),
        local_row_start,
        shared_row_block,
        0,
    )
    shared_standardized = lax.dynamic_slice_in_dim(
        first_standardized, local_row_start, shared_row_block, 0
    )
    shared_inverse_deviation = lax.dynamic_slice_in_dim(
        first_inverse_deviation, local_row_start, shared_row_block, 0
    )
    input_gradient = residual_share_gradient + norm_backward_pass(
        first_norm_gradient, shared_standardized, shared_inverse_deviation, first_norm_gain
    )
    first_gain_gradient = jnp.sum(first_norm_gradient * shared_standardized, 0)
    bias_one_grad = jnp.sum(first_norm_gradient, 0)
    grads_attn, grads_proj, grads_expand, grads_reduce = (
        lax.psum_scatter(
            grad_attn.astype(jnp.bfloat16), "grp", scatter_dimension=0, tiled=True
        ).astype(jnp.float32),
        lax.psum_scatter(
            grad_proj.astype(jnp.bfloat16), "grp", scatter_dimension=0, tiled=True
        ).astype(jnp.float32),
        lax.psum_scatter(
            grad_expand.astype(jnp.bfloat16), "grp", scatter_dimension=0, tiled=True
        ).astype(jnp.float32),
        lax.psum_scatter(
            grad_reduce.astype(jnp.bfloat16), "grp", scatter_dimension=0, tiled=True
        ).astype(jnp.float32),
    )
    small_grads = lax.psum(
        (
            query_value_full,
            bias_out_grad,
            up_bias_full,
            down_bias_grad,
            first_gain_gradient,
            bias_one_grad,
            gain_two_grad,
            bias_two_grad,
        ),
        ("grp", "tp"),
    )
    return (
        result,
        input_gradient,
        grads_attn,
        small_grads[0],
        grads_proj,
        small_grads[1],
        grads_expand,
        small_grads[2],
        grads_reduce,
        small_grads[3],
        small_grads[4],
        small_grads[5],
        small_grads[6],
        small_grads[7],
    )


def solution(mesh):
    in_specs = (
        P("grp", None),
        P("grp", None),
        P(),
        P(),
        P("grp", "tp"),
        P(),
        P("grp", "tp"),
        P(),
        P("grp", "tp"),
        P(),
        P("grp", "tp"),
        P(),
        P(),
        P(),
        P(),
        P(),
    )
    out_specs = (
        P(("grp", "tp"), None),
        P(("grp", "tp"), None),
        P("grp", "tp"),
        P(),
        P("grp", "tp"),
        P(),
        P("grp", "tp"),
        P(),
        P("grp", "tp"),
        P(),
        P(),
        P(),
        P(),
        P(),
    )
    return jax.shard_map(
        on_device, mesh=mesh, in_specs=in_specs, out_specs=out_specs, check_vma=False
    )
```

profile of v0, /device:TPU:8, one launch (start us, length us, event | category | flops | bytes accessed | tf_op | source)
XLA Modules:
  0.0 1345.7 jit_solution(15598600205464487332)
XLA Ops:
  13.4 4.7 convert_reduce_fusion
  21.6 34.0 %all-gather.5.cloned.1.call-done = bf16[2048,768]{1,0:T(8,128)(2,1)} async-done(((bf16[512,768]{1,0:T(8,128)(2,1)}), bf16[2048,768]{1,0:T(8,128)(2,1)}) %all-gather.5.cloned.1.call-update) | async-done | bytes 3145744 | tf_op jit(solution)/shard_map/all_gather | solution.py:54
  55.6 11.5 add_convert_fusion.2
  71.4 46.1 %while.28 = (s32[]{:T(128)}, bf16[4,512,2,128]{3,2,1,0:T(2,128)(2,1)}, f32[4,2,512]{2,1,0:T(2,128)}, s32[4]{0:T(128)S(1)}, s32[2048]{0:T(1024)S(1)}, /*index=5*/...) while((s32[]{:T(128)}, ...), condition=%wide.region_7.8_spmd.clone, body=%wide.region_4.7_spmd.clone.sunk | while | flops 1102183936 | bytes 32557260 | solution.py:129
  75.9 2.5 fusion.135
  78.4 2.9 fusion.136
  87.4 2.5 fusion.135
  89.9 2.9 fusion.136
  98.9 2.5 fusion.135
  101.4 2.9 fusion.136
  110.4 2.5 fusion.135
  112.9 2.9 fusion.136
  117.5 8.2 convolution_convert_fusion.3
  125.9 2.7 convert_element_type.139
  128.7 2.7 convert_element_type.141
  132.2 169.3 %all-reduce.7.cloned.1.call-done = bf16[2048,2048]{1,0:T(8,128)(2,1)} async-done(((bf16[2048,2048]{1,0:T(8,128)(2,1)}), bf16[2048,2048]{1,0:T(8,128)(2,1)}) %all-reduce.7.cloned.1.call-update) | async-done | bytes 8388624 | tf_op jit(solution)/shard_map/psum | solution.py:131
  301.5 17.6 %fusion.88 = (f32[2048]{0:T(1024)S(1)}, f32[2048,2048]{1,0:T(8,128)}, f32[2048,2048]{1,0:T(8,128)}) fusion(f32[2048]{0:T(1024)S(1)} %copy-done.25, bf16[2048,2048]{1,0:T(8,128)(2,1)} %all-reduce.7.cloned.1.call-done, bf16[2048,2048]{1,0:T(8,128)(2,1)} %param.20, f32[2048]{0:T(1024)S(1)} %add_rsqrt_fusion.1, f32[2048]{0:T(1024)S(1)} %broadcast_multiply_fusion.3), kind=kLoop, calls=%fused_computation.141 | loop fusion | flops 29358080 | bytes 50364416 | tf_op jit(solution)/shard_map/reduce_sum | solution.py:10
  319.1 7.6 multiply_reduce_fusion.2
  326.7 11.8 subtract_multiply_fusion
  338.5 18.2 %all-gather.9.cloned.1.call-done = bf16[2048,1024]{1,0:T(8,128)(2,1)} async-done(((bf16[512,1024]{1,0:T(8,128)(2,1)}), bf16[2048,1024]{1,0:T(8,128)(2,1)}) %all-gather.9.cloned.1.call-update) | async-done | bytes 4194320 | tf_op jit(solution)/shard_map/all_gather | solution.py:56
  356.7 15.5 %fusion.75 = f32[2048,1024]{1,0:T(8,128)} fusion(bf16[2048,1024]{1,0:T(8,128)(2,1)} %all-gather.9.cloned.1.call-done, f32[2048,2048]{1,0:T(8,128)} %subtract_multiply_fusion, f32[2048]{0:T(1024)S(1)} %copy-done.31, f32[2048]{0:T(1024)S(1)} %copy-done.21), kind=kOutput, calls=%fused_computation.102 | convolution fusion | flops 8602517504 | bytes 29376512 | tf_op jit(solution)/shard_map/dot_general | solution.py:140
  372.2 39.5 %all-gather.11.cloned.1.call-done = bf16[2048,1024]{1,0:T(8,128)(2,1)} async-done(((bf16[512,1024]{1,0:T(8,128)(2,1)}), bf16[2048,1024]{1,0:T(8,128)(2,1)}) %all-gather.11.cloned.1.call-update) | async-done | bytes 4194320 | tf_op jit(solution)/shard_map/all_gather | solution.py:57
  411.7 19.5 %convert_reduce_fusion.1 = (f32[1024]{0:T(1024)}, bf16[2048,1024]{1,0:T(8,128)(2,1)S(1)}) fusion(f32[2048,1024]{1,0:T(8,128)} %fusion.75, f32[1024]{0:T(1024)S(1)} %dynamic_slice.59, bf16[2048,1024]{1,0:T(8,128)(2,1)} %all-gather.11.cloned.1.call-done, f32[2048]{0:T(1024)S(1)} %compare_convert_fusion, bf16[2048,2048]{1,0:T(8,128)(2,1)} %param.21), kind=kOutput, calls=%fused_computation.74 | convolution fusion | flops 8650750976 | bytes 25182208 | tf_op jit(solution)/shard_map/dot_general | solution.py:156
  433.2 10.9 convolution_convert_fusion.1
  444.1 175.7 %all-reduce.9.cloned.1.call-done = bf16[2048,2048]{1,0:T(8,128)(2,1)} async-done(((bf16[2048,2048]{1,0:T(8,128)(2,1)}), bf16[2048,2048]{1,0:T(8,128)(2,1)}) %all-reduce.9.cloned.1.call-update) | async-done | bytes 8388624 | tf_op jit(solution)/shard_map/psum | solution.py:161
  619.8 10.5 multiply_reduce_fusion.3
  630.3 19.1 %convert_multiply_fusion = (f32[2048,2048]{1,0:T(8,128)}, f32[2048,2048]{1,0:T(8,128)S(1)}) fusion(bf16[2048,2048]{1,0:T(8,128)(2,1)} %param.21, f32[2048]{0:T(1024)S(1)} %compare_convert_fusion, f32[2048]{0:T(1024)S(1)} %broadcast_multiply_fusion, f32[2048]{0:T(1024)S(1)} %broadcast_multiply_fusion.1, f32[2048]{0:T(1024)S(1)} %copy-done.21, ...), kind=kLoop, calls=%fused_computation.59 | loop fusion | flops 46137344 | bytes 67158016 | tf_op jit(solution)/shard_map/mul | solution.py:152
  649.4 5.7 copy-done
  655.1 3.6 fusion.70
  658.8 16.8 %fusion.61 = bf16[2048,1024]{1,0:T(8,128)(2,1)} fusion(bf16[2048,2048]{1,0:T(8,128)(2,1)} %param.21, f32[2048]{0:T(1024)S(1)} %compare_convert_fusion, f32[2048,1024]{1,0:T(8,128)} %fusion.75, f32[1024]{0:T(1024)S(1)} %dynamic_slice.59), kind=kOutput, calls=%fused_computation.91 | convolution fusion | flops 8625586176 | bytes 20983808 | tf_op jit(solution)/shard_map/dot_general | solution.py:26
  675.7 15.3 %convolution_convert_fusion.4 = bf16[2048,1024]{1,0:T(8,128)(2,1)} fusion(bf16[2048,1024]{1,0:T(8,128)(2,1)} %copy-done.34, f32[2048,2048]{1,0:T(8,128)} %subtract_multiply_fusion, f32[2048]{0:T(1024)S(1)} %copy-done.31, f32[2048]{0:T(1024)S(1)} %copy-done.21), kind=kOutput, calls=%fused_computation.92 | convolution fusion | flops 8604614656 | bytes 25182208 | tf_op jit(solution)/shard_map/dot_general | solution.py:26
  691.1 9.8 fusion.67
  700.9 89.8 %while.29 = (s32[]{:T(128)}, f32[2048,2,128]{0,2,1:T(8,128)S(1)}, f32[2048,2,128]{0,2,1:T(8,128)}, bf16[4,512,2,128]{3,1,0,2:T(8,128)(2,1)}, s32[4]{0:T(128)S(1)...) while((s32[]{:T(128)}, f32[2048,2,128]{0,2,1:T(8,128)S(1)}, ...), condition=%wide.region_17.18_spmd.clone, body=%wide.region_15.17_spmd.clone.sunk | while | flops 2721709568 | bytes 97040784 | solution.py:220
  708.6 3.7 fusion.149
  712.3 3.8 multiply_reduce_fusion.6
  716.2 2.6 multiply_convert_fusion.6
  720.1 2.4 fusion.148
  730.1 5.0 fusion.149
  735.1 3.9 multiply_reduce_fusion.6
  739.0 2.6 multiply_convert_fusion.6
  742.9 2.4 fusion.148
  752.8 5.0 fusion.149
  757.8 3.8 multiply_reduce_fusion.6
  761.7 2.6 multiply_convert_fusion.6
  765.6 2.4 fusion.148
  775.5 5.0 fusion.149
  780.5 3.9 multiply_reduce_fusion.6
  784.4 2.6 multiply_convert_fusion.6
  788.3 2.4 fusion.148
  792.1 2.7 copy.79
  797.2 2.9 copy.80
  800.1 13.1 convolution_convert_fusion.5
  813.2 17.8 %convolution_convert_fusion.2 = bf16[2048,2048]{1,0:T(8,128)(2,1)} fusion(bf16[2048,1024]{1,0:T(8,128)(2,1)} %all-gather.11.cloned.1.call-done, f32[2048,1024]{1,0:T(8,128)} %fusion.75, f32[1024]{0:T(1024)S(1)} %copy-done.28), kind=kOutput, calls=%fused_computation.78 | convolution fusion | flops 8615100416 | bytes 20975616 | tf_op jit(solution)/shard_map/dot_general | solution.py:26
  831.1 9.2 convolution_convert_fusion
  841.7 11.3 convert_element_type.149
  855.3 3.2 dynamic-slice_reduce_fusion.1
  860.4 2.8 convert_element_type.165
  863.2 2.8 convert_element_type.162
  866.0 2.5 convert_element_type.157
  868.6 325.1 %all-reduce.13.cloned.1.call-done = (bf16[2048,2048]{1,0:T(8,128)(2,1)}, bf16[2048,2048]{1,0:T(8,128)(2,1)}) async-done(((bf16[2048,2048]{1,0:T(8,128)(2,1)}, bf16[2048,2048]{1,0:T(8,128)(2,1)}), (bf16[2048,2048]{1,0:T(8,128)(2,1)}, bf16[2048,2048]{1,0:T(8,128)(2,1)})) %all-reduce.13.cloned.1.call-update) | async-done | bytes 16777232 | tf_op jit(solution)/shard_map/psum | solution.py:143
  1193.6 3.2 fusion.79
  1196.9 5.2 dynamic-slice_reduce_fusion.2
  1202.1 3.2 multiply_convert_fusion.2
  1205.3 122.7 %all-reduce.11.cloned.1.call-done = (f32[4096]{0:T(1024)}, f32[2048]{0:T(1024)}, f32[8192]{0:T(1024)}, f32[2048]{0:T(1024)}, f32[2048]{0:T(1024)}, /*index=5*/f32[2048]{0:T(1024)}, f32[2048]{0:T(1024)}, f32[2048]{0:T(1024)}) async-done(((f32[4096]{0:T(1024)}, f32[2048]{0:T(1024)}, f32[8192]{0:T(1024)}, f32[2048]{0:T(1024)}, f32[2048]{0:T(1024)}, /*index=5*/f32[2048]{0:T(1024)}, f32[2048]{0:T(1024)}, ...) | async-done | bytes 98320 | tf_op jit(solution)/shard_map/psum | solution.py:274
  (231 shorter events, 83.4 us)
Async XLA Ops:
  7.2 48.4 %all-gather.5.cloned.1.call-start = ((), (), s32[]{:S(2)}) async-start(), calls=%async_computation.4 | async-start | bytes 3932160 | tf_op jit(solution)/shard_map/all_gather | solution.py:54
  9.6 107.9 %all-gather.7.cloned.1.call-start = ((), (), s32[]{:S(2)}) async-start(), calls=%async_computation.5 | async-start | bytes 1310720 | tf_op jit(solution)/shard_map/all_gather | solution.py:55
  11.5 290.1 %all-reduce.7.cloned.1.call-start = ((), (), s32[]{:S(2)}) async-start(), calls=%async_computation.6 | async-start | bytes 16777216 | tf_op jit(solution)/shard_map/psum | solution.py:131
  13.3 6.0 copy-start.3
  13.4 42.2 %copy-start.22 = (f32[2048]{0:T(1024)S(1)}, f32[2048]{0:T(1024)}, u32[]{:S(2)}) copy-start(f32[2048]{0:T(1024)} %param.32) | copy-start | bytes 24580
  13.4 42.2 %copy-start.32 = (f32[2048]{0:T(1024)S(1)}, f32[2048]{0:T(1024)}, u32[]{:S(2)}) copy-start(f32[2048]{0:T(1024)} %param.33) | copy-start | bytes 24580
  19.2 282.3 %copy-start.15 = (f32[2048]{0:T(1024)}, f32[2048]{0:T(1024)S(1)}, u32[]{:S(2)}) copy-start(f32[2048]{0:T(1024)S(1)} %broadcast_multiply_fusion.3) | copy-start | bytes 24580
  21.6 280.0 %copy-start.19 = (f32[2048]{0:T(1024)}, f32[2048]{0:T(1024)S(1)}, u32[]{:S(2)}) copy-start(f32[2048]{0:T(1024)S(1)} %add_rsqrt_fusion.1) | copy-start | bytes 24580
  117.5 8.3 copy-start.1
  117.5 8.3 copy-start.4
  117.5 8.3 copy-start.6
  117.5 8.3 copy-start.10
  125.8 175.8 %copy-start.25 = (f32[2048]{0:T(1024)S(1)}, f32[2048]{0:T(1024)}, u32[]{:S(2)}) copy-start(f32[2048]{0:T(1024)} %param.27) | copy-start | bytes 24580
  125.8 230.8 %all-gather.9.cloned.1.call-start = ((), (), s32[]{:S(2)}) async-start(), calls=%async_computation.7 | async-start | bytes 5242880 | tf_op jit(solution)/shard_map/all_gather | solution.py:56
  128.6 283.0 %all-gather.11.cloned.1.call-start = ((), (), s32[]{:S(2)}) async-start(), calls=%async_computation.8 | async-start | bytes 5242880 | tf_op jit(solution)/shard_map/all_gather | solution.py:57
  131.4 488.4 %all-reduce.9.cloned.1.call-start = ((), (), s32[]{:S(2)}) async-start(), calls=%async_computation.9 | async-start | bytes 16777216 | tf_op jit(solution)/shard_map/psum | solution.py:161
  131.5 527.3 %copy-start.18 = (f32[2048]{0:T(1024)}, f32[2048]{0:T(1024)S(1)}, u32[]{:S(2)}) copy-start(f32[2048]{0:T(1024)S(1)} %compare_convert_fusion) | copy-start | bytes 24580
  132.2 526.6 %copy-start.27 = (f32[1024]{0:T(1024)}, f32[1024]{0:T(1024)S(1)}, u32[]{:S(2)}) copy-start(f32[1024]{0:T(1024)S(1)} %dynamic_slice.59) | copy-start | bytes 12292
  326.7 30.0 %copy-start.21 = (f32[2048]{0:T(1024)S(1)}, f32[2048]{0:T(1024)}, u32[]{:S(2)}) copy-start(f32[2048]{0:T(1024)} %param.34) | copy-start | bytes 24580
  326.7 30.0 %copy-start.31 = (f32[2048]{0:T(1024)S(1)}, f32[2048]{0:T(1024)}, u32[]{:S(2)}) copy-start(f32[2048]{0:T(1024)} %param.35) | copy-start | bytes 24580
  411.7 21.5 %copy-start.29 = (bf16[2048,1024]{1,0:T(8,128)(2,1)S(1)}, bf16[2048,1024]{1,0:T(8,128)(2,1)}, u32[]{:S(2)}) copy-start(bf16[2048,1024]{1,0:T(8,128)(2,1)} %all-gather.9.cloned.1.call-done) | copy-start | bytes 12582916
  431.2 2.0 copy-start.34
  444.1 414.6 %reduce-scatter.7.cloned.1.call-start = ((), (), s32[]{:S(2)}) async-start(), calls=%async_computation.11 | async-start | bytes 1310720 | tf_op jit(solution)/shard_map/reduce_scatter | solution.py:264
  630.3 24.8 %copy-start.8 = (bf16[4,512,2,128]{3,2,1,0:T(2,128)(2,1)S(1)}, bf16[4,512,2,128]{3,2,1,0:T(2,128)(2,1)}, u32[]{:S(2)}) copy-start(bf16[4,512,2,128]{3,2,1,0:T(2,128)(2,1)} %get-tuple-element.126) | copy-start | bytes 3145732
  649.4 5.7 copy-start
  658.7 201.7 %reduce-scatter.11.cloned.1.call-start = ((), (), s32[]{:S(2)}) async-start(), calls=%async_computation.13 | async-start | bytes 5242880 | tf_op jit(solution)/shard_map/reduce_scatter | solution.py:270
  675.7 187.6 %reduce-scatter.9.cloned.1.call-start = ((), (), s32[]{:S(2)}) async-start(), calls=%async_computation.12 | async-start | bytes 5242880 | tf_op jit(solution)/shard_map/reduce_scatter | solution.py:267
  691.1 9.8 copy-start.2
  691.1 9.8 copy-start.11
  691.1 174.9 %reduce-scatter.5.cloned.1.call-start = ((), (), s32[]{:S(2)}) async-start(), calls=%async_computation.10 | async-start | bytes 3932160 | tf_op jit(solution)/shard_map/reduce_scatter | solution.py:261
  704.3 4.3 copy-start.7
  708.6 3.7 copy-start.5
  716.2 2.6 copy-start.12
  720.1 2.4 copy-start.13
  725.7 4.4 copy-start.7
  730.1 5.0 copy-start.5
  739.0 2.6 copy-start.12
  742.9 2.4 copy-start.13
  748.5 4.3 copy-start.7
  752.8 5.0 copy-start.5
  761.7 2.6 copy-start.12
  765.6 2.4 copy-start.13
  771.2 4.3 copy-start.7
  775.5 5.0 copy-start.5
  784.4 2.6 copy-start.12
  788.3 2.4 copy-start.13
  792.1 7.9 copy-start.16
  792.1 7.9 copy-start.20
  792.1 7.9 copy-start.23
  792.1 7.9 copy-start.33
  800.1 13.2 copy-start.28
  813.2 17.9 %copy-start.9 = (bf16[2048,2,3,128]{0,3,2,1:T(8,128)(2,1)S(1)}, bf16[2048,2,3,128]{0,3,2,1:T(8,128)(2,1)}, u32[]{:S(2)}) copy-start(bf16[2048,2,3,128]{0,3,2,1:T(8,128)(2,1)} %copy.80) | copy-start | bytes 9437188
  813.2 380.5 %all-reduce.13.cloned.1.call-start = ((), (), s32[]{:S(2)}) async-start(), calls=%async_computation.15 | async-start | bytes 33554432 | tf_op jit(solution)/shard_map/psum | solution.py:143
  813.2 17.8 %copy-start.30 = (bf16[2048,768]{1,0:T(8,128)(2,1)S(1)}, bf16[2048,768]{1,0:T(8,128)(2,1)}, u32[]{:S(2)}) copy-start(bf16[2048,768]{1,0:T(8,128)(2,1)} %all-gather.5.cloned.1.call-done) | copy-start | bytes 9437188
  840.2 0.9 copy-start.26
  840.2 487.7 %all-reduce.11.cloned.1.call-start = ((), (), s32[]{:S(2)}) async-start(), calls=%async_computation.14 | async-start | bytes 196608 | tf_op jit(solution)/shard_map/psum | solution.py:274
  841.7 11.3 copy-start.14
  858.6 343.5 %copy-start.17 = (f32[16,2,128]{2,1,0:T(2,128)}, f32[16,2,128]{2,1,0:T(2,128)S(1)}, u32[]{:S(2)}) copy-start(f32[16,2,128]{2,1,0:T(2,128)S(1)} %constant_dynamic-update-slice_fusion) | copy-start | bytes 49156
  863.2 338.9 %copy-start.24 = (f32[2048]{0:T(1024)S(1)}, f32[2048]{0:T(1024)}, u32[]{:S(2)}) copy-start(f32[2048]{0:T(1024)} %param.31) | copy-start | bytes 24580
Sparse Core Ops, SparseCore 0:
  10.4 45.1 all-gather.4
  58.0 26.6 all-gather.6
  125.9 175.5 all-reduce.6
  303.8 52.8 all-gather.8
  358.9 52.6 all-gather.10
  444.2 175.5 all-reduce.8
  658.8 27.8 reduce-scatter.6
  690.0 52.6 reduce-scatter.10
  745.7 52.6 reduce-scatter.8
  813.3 43.9 reduce-scatter.4
  860.1 333.5 all-reduce.12
  1202.2 125.6 all-reduce.10
where the time goes:
time: 1350 us
  waiting for transfers between devices  885 us (66%)
  matrix products  229 us (17%)
  other arithmetic  157 us (12%)
  local copies, waits for them, and re-layouts  45.9 us (3%)
  between operations  15.2 us (1%)
  loops' own time  14 us (1%)
    psum x1, waiting for transfers between devices, on_device(): lax.psum(contract(active, w_reduce, 1, 1).astype(jnp.bfloat16), 'tp')  325 us
    psum x1, waiting for transfers between devices, on_device(): lax.psum(contract(grad_beforeb, w_expand, 1, 1).astype(jnp.bfloat16), 'tp')  176 us
    psum x1, waiting for transfers between devices, on_device(): lax.psum(contract(context_all, w_proj, 1, 1).astype(jnp.bfloat16), 'tp')  169 us
    psum x1, waiting for transfers between devices, on_device(): lax.psum((query_value_full, bias_out_grad, up_bias_full, down_bias_grad,...  123 us
    dot_general x8, matrix products, contract(): lax.dot_general(left, right, (((left_dim,), (right_dim,)), ((), ())), pre...  94.9 us
    all_gather x1, waiting for transfers between devices, on_device(): lax.all_gather(w_down.astype(jnp.bfloat16), 'grp', axis=0, tiled=True)  39.5 us
    all_gather x1, waiting for transfers between devices, on_device(): lax.all_gather(w_qkv.astype(jnp.bfloat16), 'grp', axis=0, tiled=True)  34 us
  transfers between devices with their start and end apart: 12, of which 7 were waited for; matrix products, arithmetic and copies ran while one was open for 24% of the time, Pallas kernels for 0%

commit v1 on v0

--- a/solution.py
+++ b/solution.py
@@ -4,6 +4,27 @@
 from jax.sharding import PartitionSpec as P
 
 HD = 128
+
+
+def ring_gather(x, axis, dim):
+    size, index, extent = (lax.axis_size(axis), lax.axis_index(axis), x.shape[dim])
+    right = [(i, (i + 1) % size) for i in range(size)]
+    left = [(i, (i - 1) % size) for i in range(size)]
+    whole = jnp.zeros((*x.shape[:dim], size * extent, *x.shape[dim + 1 :]), x.dtype)
+    whole = lax.dynamic_update_slice_in_dim(whole, x, index * extent, axis=dim)
+    from_left = from_right = x
+    middle = size // 2
+    for lap in range(1, middle + 1):
+        from_left = lax.ppermute(from_left, axis, right)
+        whole = lax.dynamic_update_slice_in_dim(
+            whole, from_left, (index - lap) % size * extent, axis=dim
+        )
+        if lap < size - middle:
+            from_right = lax.ppermute(from_right, axis, left)
+            whole = lax.dynamic_update_slice_in_dim(
+                whole, from_right, (index + lap) % size * extent, axis=dim
+            )
+    return whole
 
 
 def layer_normalize(rows, gain, bias):
@@ -54,7 +75,7 @@
         lax.all_gather(w_qkv.astype(jnp.bfloat16), "grp", axis=0, tiled=True),
         lax.all_gather(w_out.astype(jnp.bfloat16), "grp", axis=0, tiled=True),
         lax.all_gather(w_up.astype(jnp.bfloat16), "grp", axis=0, tiled=True),
-        lax.all_gather(w_down.astype(jnp.bfloat16), "grp", axis=0, tiled=True),
+        ring_gather(w_down.astype(jnp.bfloat16), "grp", 0),
     )
     tp_rank = lax.axis_index("tp")
     tp_count = lax.axis_size("tp")

time: 1350 us -> 1310 us (0.970)
  waiting for transfers between devices: 885 us -> 836 us
    psum x1, waiting for transfers between devices: 169 us -> 98.4 us  [on_device(): lax.psum(contract(context_all, w_proj, 1, 1).astype(jnp.bfloat16), 'tp')]
    ppermute x0 -> x3, waiting for transfers between devices: none -> 62 us  [the longest x2 43.2 us: ring_gather(): from_left = lax.ppermute(from_left, axis, right)]
    all_gather x1 -> x0, waiting for transfers between devices: 39.5 us -> none  [on_device(): lax.all_gather(w_down.astype(jnp.bfloat16), 'grp', axis=0, tiled=True)]
  transfers between devices with their start and end apart: 12 -> 14, of which waited for: 7 -> 9; matrix products, arithmetic and copies ran while one was open for 24% -> 24% of each run, Pallas kernels for 0% -> 0%
where the time goes in v1:
time: 1310 us
  waiting for transfers between devices  836 us (64%)
  matrix products  228 us (17%)
  other arithmetic  156 us (12%)
  local copies, waits for them, and re-layouts  52.8 us (4%)
  between operations  14.9 us (1%)
  loops' own time  14 us (1%)
    psum x1, waiting for transfers between devices, on_device(): lax.psum(contract(active, w_reduce, 1, 1).astype(jnp.bfloat16), 'tp')  325 us
    psum x1, waiting for transfers between devices, on_device(): lax.psum(contract(grad_beforeb, w_expand, 1, 1).astype(jnp.bfloat16), 'tp')  176 us
    psum x1, waiting for transfers between devices, on_device(): lax.psum((query_value_full, bias_out_grad, up_bias_full, down_bias_grad,...  123 us
    psum x1, waiting for transfers between devices, on_device(): lax.psum(contract(context_all, w_proj, 1, 1).astype(jnp.bfloat16), 'tp')  98.4 us
    dot_general x8, matrix products, contract(): lax.dot_general(left, right, (((left_dim,), (right_dim,)), ((), ())), pre...  94.9 us
    ppermute x2, waiting for transfers between devices, ring_gather(): from_left = lax.ppermute(from_left, axis, right)  43.2 us
    all_gather x1, waiting for transfers between devices, on_device(): lax.all_gather(w_qkv.astype(jnp.bfloat16), 'grp', axis=0, tiled=True)  34 us
  transfers between devices with their start and end apart: 14, of which 9 were waited for; matrix products, arithmetic and copies ran while one was open for 24% of the time, Pallas kernels for 0%

profile of v1, /device:TPU:8, one launch (start us, length us, event | category | flops | bytes accessed | tf_op | source)
XLA Modules:
  0.0 1305.5 jit_solution(8149133300228723358)
XLA Ops:
  13.4 4.7 convert_reduce_fusion
  21.6 34.0 %all-gather.4.cloned.1.call-done = bf16[2048,768]{1,0:T(8,128)(2,1)} async-done(((bf16[512,768]{1,0:T(8,128)(2,1)}), bf16[2048,768]{1,0:T(8,128)(2,1)}) %all-gather.4.cloned.1.call-update) | async-done | bytes 3145744 | tf_op jit(solution)/shard_map/all_gather | solution.py:75
  55.6 11.5 add_convert_fusion.2
  71.4 46.1 %while.28 = (s32[]{:T(128)}, bf16[4,512,2,128]{3,2,1,0:T(2,128)(2,1)}, f32[4,2,512]{2,1,0:T(2,128)}, s32[4]{0:T(128)S(1)}, s32[2048]{0:T(1024)S(1)}, /*index=5*/...) while((s32[]{:T(128)}, ...), condition=%wide.region_7.8_spmd.clone, body=%wide.region_4.7_spmd.clone.sunk | while | flops 1102183936 | bytes 32557260 | solution.py:150
  75.9 2.5 fusion.135
  78.4 2.9 fusion.136
  87.4 2.5 fusion.135
  89.9 2.9 fusion.136
  98.9 2.5 fusion.135
  101.4 2.9 fusion.136
  110.4 2.5 fusion.135
  112.9 2.9 fusion.136
  117.5 8.2 convolution_convert_fusion.3
  125.9 2.5 broadcast_in_dim.126
  128.4 2.9 constant_dynamic-update-slice_fusion.4
  135.6 22.9 %collective-permute-done = bf16[512,1024]{1,0:T(8,128)(2,1)} collective-permute-done((bf16[512,1024]{1,0:T(8,128)(2,1)S(1)}, bf16[512,1024]{1,0:T(8,128)(2,1)}, u32[]{:S(2)}, u32[]{:S(2)}) %collective-permute-start) | collective-permute-done | bytes 1048608 | tf_op jit(solution)/shard_map/ppermute | solution.py:18
  161.9 18.8 %collective-permute-done.1 = bf16[512,1024]{1,0:T(8,128)(2,1)S(1)} collective-permute-done((bf16[512,1024]{1,0:T(8,128)(2,1)S(1)}, bf16[512,1024]{1,0:T(8,128)(2,1)S(1)}, u32[]{:S(2)}, u32[]{:S(2)}) %collective-permute-start.1) | collective-permute-done | bytes 1048608 | tf_op jit(solution)/shard_map/ppermute | solution.py:23
  181.7 20.4 %collective-permute-done.2 = bf16[512,1024]{1,0:T(8,128)(2,1)S(1)} collective-permute-done((bf16[512,1024]{1,0:T(8,128)(2,1)}, bf16[512,1024]{1,0:T(8,128)(2,1)S(1)}, u32[]{:S(2)}, u32[]{:S(2)}) %collective-permute-start.2) | collective-permute-done | bytes 1048608 | tf_op jit(solution)/shard_map/ppermute | solution.py:18
  203.2 98.4 %all-reduce.7.cloned.1.call-done = bf16[2048,2048]{1,0:T(8,128)(2,1)} async-done(((bf16[2048,2048]{1,0:T(8,128)(2,1)}), bf16[2048,2048]{1,0:T(8,128)(2,1)}) %all-reduce.7.cloned.1.call-update) | async-done | bytes 8388624 | tf_op jit(solution)/shard_map/psum | solution.py:152
  301.5 17.6 %fusion.88 = (f32[2048]{0:T(1024)S(1)}, f32[2048,2048]{1,0:T(8,128)}, f32[2048,2048]{1,0:T(8,128)}) fusion(f32[2048]{0:T(1024)S(1)} %copy-done.26, bf16[2048,2048]{1,0:T(8,128)(2,1)} %all-reduce.7.cloned.1.call-done, bf16[2048,2048]{1,0:T(8,128)(2,1)} %param.20, f32[2048]{0:T(1024)S(1)} %add_rsqrt_fusion.1, f32[2048]{0:T(1024)S(1)} %broadcast_multiply_fusion.3), kind=kLoop, calls=%fused_computation.145 | loop fusion | flops 29358080 | bytes 50364416 | tf_op jit(solution)/shard_map/reduce_sum | solution.py:31
  319.1 7.6 multiply_reduce_fusion.2
  326.7 11.8 subtract_multiply_fusion
  338.5 18.1 %all-gather.8.cloned.1.call-done = bf16[2048,1024]{1,0:T(8,128)(2,1)} async-done(((bf16[512,1024]{1,0:T(8,128)(2,1)}), bf16[2048,1024]{1,0:T(8,128)(2,1)}) %all-gather.8.cloned.1.call-update) | async-done | bytes 4194320 | tf_op jit(solution)/shard_map/all_gather | solution.py:77
  356.7 13.2 %fusion.75 = f32[2048,1024]{1,0:T(8,128)S(1)} fusion(bf16[2048,1024]{1,0:T(8,128)(2,1)} %all-gather.8.cloned.1.call-done, f32[2048,2048]{1,0:T(8,128)} %subtract_multiply_fusion, f32[2048]{0:T(1024)S(1)} %copy-done.32, f32[2048]{0:T(1024)S(1)} %copy-done.22), kind=kOutput, calls=%fused_computation.102 | convolution fusion | flops 8602517504 | bytes 29376512 | tf_op jit(solution)/shard_map/dot_general | solution.py:161
  369.9 21.4 %convert_reduce_fusion.1 = (f32[1024]{0:T(1024)}, bf16[2048,1024]{1,0:T(8,128)(2,1)S(1)}) fusion(f32[2048,1024]{1,0:T(8,128)S(1)} %fusion.75, f32[1024]{0:T(1024)S(1)} %dynamic_slice.59, bf16[2048,1024]{1,0:T(8,128)(2,1)} %constant_dynamic-update-slice_fusion.1, f32[2048]{0:T(1024)S(1)} %compare_convert_fusion, bf16[2048,2048]{1,0:T(8,128)(2,1)} %param.21), kind=kOutput, calls=%fused_computation.74 | convolution fusion | flops 8650750976 | bytes 25182208 | tf_op jit(solution)/shard_map/dot_general | solution.py:177
  393.2 10.9 convolution_convert_fusion.1
  404.2 175.7 %all-reduce.9.cloned.1.call-done = bf16[2048,2048]{1,0:T(8,128)(2,1)} async-done(((bf16[2048,2048]{1,0:T(8,128)(2,1)}), bf16[2048,2048]{1,0:T(8,128)(2,1)}) %all-reduce.9.cloned.1.call-update) | async-done | bytes 8388624 | tf_op jit(solution)/shard_map/psum | solution.py:182
  579.9 10.5 multiply_reduce_fusion.3
  590.4 19.1 %convert_multiply_fusion = (f32[2048,2048]{1,0:T(8,128)}, f32[2048,2048]{1,0:T(8,128)S(1)}) fusion(bf16[2048,2048]{1,0:T(8,128)(2,1)} %param.21, f32[2048]{0:T(1024)S(1)} %compare_convert_fusion, f32[2048]{0:T(1024)S(1)} %broadcast_multiply_fusion, f32[2048]{0:T(1024)S(1)} %broadcast_multiply_fusion.1, f32[2048]{0:T(1024)S(1)} %copy-done.22, ...), kind=kLoop, calls=%fused_computation.59 | loop fusion | flops 46137344 | bytes 67158016 | tf_op jit(solution)/shard_map/mul | solution.py:173
  609.5 5.7 copy-done
  615.2 3.6 fusion.70
  618.9 16.8 %fusion.61 = bf16[2048,1024]{1,0:T(8,128)(2,1)} fusion(bf16[2048,2048]{1,0:T(8,128)(2,1)} %param.21, f32[2048]{0:T(1024)S(1)} %compare_convert_fusion, f32[2048,1024]{1,0:T(8,128)} %copy-done.35, f32[1024]{0:T(1024)S(1)} %dynamic_slice.59), kind=kOutput, calls=%fused_computation.91 | convolution fusion | flops 8625586176 | bytes 20983808 | tf_op jit(solution)/shard_map/dot_general | solution.py:47
  635.9 15.3 %convolution_convert_fusion.4 = bf16[2048,1024]{1,0:T(8,128)(2,1)} fusion(bf16[2048,1024]{1,0:T(8,128)(2,1)} %copy-done.36, f32[2048,2048]{1,0:T(8,128)} %subtract_multiply_fusion, f32[2048]{0:T(1024)S(1)} %copy-done.32, f32[2048]{0:T(1024)S(1)} %copy-done.22), kind=kOutput, calls=%fused_computation.92 | convolution fusion | flops 8604614656 | bytes 25182208 | tf_op jit(solution)/shard_map/dot_general | solution.py:47
  651.3 9.8 fusion.67
  661.0 89.8 %while.29 = (s32[]{:T(128)}, f32[2048,2,128]{0,2,1:T(8,128)S(1)}, f32[2048,2,128]{0,2,1:T(8,128)}, bf16[4,512,2,128]{3,1,0,2:T(8,128)(2,1)}, s32[4]{0:T(128)S(1)...) while((s32[]{:T(128)}, f32[2048,2,128]{0,2,1:T(8,128)S(1)}, ...), condition=%wide.region_17.18_spmd.clone, body=%wide.region_15.17_spmd.clone.sunk | while | flops 2721709568 | bytes 97040784 | solution.py:241
  668.7 3.7 fusion.149
  672.5 3.9 multiply_reduce_fusion.6
  676.3 2.6 multiply_convert_fusion.6
  690.2 5.0 fusion.149
  695.2 3.9 multiply_reduce_fusion.6
  699.1 2.6 multiply_convert_fusion.6
  703.0 2.4 fusion.148
  712.9 5.0 fusion.149
  718.0 3.8 multiply_reduce_fusion.6
  721.8 2.6 multiply_convert_fusion.6
  735.6 5.0 fusion.149
  740.6 3.9 multiply_reduce_fusion.6
  744.5 2.6 multiply_convert_fusion.6
  748.4 2.4 fusion.148
  752.2 2.7 copy.79
  757.3 2.9 copy.80
  760.2 13.1 %convolution_convert_fusion.5 = bf16[2048,768]{1,0:T(8,128)(2,1)} fusion(bf16[2048,768]{0,1:T(8,128)(2,1)} %bitcast.102, f32[2048]{0:T(1024)S(1)} %copy-done.34, f32[2048]{0:T(1024)S(1)} %copy-done.24, bf16[2048,2048]{1,0:T(8,128)(2,1)} %param.20, f32[2048]{0:T(1024)S(1)} %copy-done.21, f32[2048]{0:T(1024)S(1)} %copy-done.17), kind=kOutput, calls=%fused_computation.93 | convolution fusion | flops 6469189632 | bytes 14712832 | tf_op jit(solution)/shard_map/dot_general | solution.py:47
  773.4 17.8 %convolution_convert_fusion.2 = bf16[2048,2048]{1,0:T(8,128)(2,1)} fusion(bf16[2048,1024]{1,0:T(8,128)(2,1)} %constant_dynamic-update-slice_fusion.1, f32[2048,1024]{1,0:T(8,128)} %copy-done.35, f32[1024]{0:T(1024)S(1)} %copy-done.28), kind=kOutput, calls=%fused_computation.78 | convolution fusion | flops 8615100416 | bytes 20975616 | tf_op jit(solution)/shard_map/dot_general | solution.py:47
  791.2 9.1 convolution_convert_fusion
  801.8 11.3 convert_element_type.149
  815.5 3.2 dynamic-slice_reduce_fusion.1
  820.5 2.8 convert_element_type.165
  823.3 2.8 convert_element_type.162
  826.1 2.5 convert_element_type.157
  828.6 325.0 %all-reduce.13.cloned.1.call-done = (bf16[2048,2048]{1,0:T(8,128)(2,1)}, bf16[2048,2048]{1,0:T(8,128)(2,1)}) async-done(((bf16[2048,2048]{1,0:T(8,128)(2,1)}, bf16[2048,2048]{1,0:T(8,128)(2,1)}), (bf16[2048,2048]{1,0:T(8,128)(2,1)}, bf16[2048,2048]{1,0:T(8,128)(2,1)})) %all-reduce.13.cloned.1.call-update) | async-done | bytes 16777232 | tf_op jit(solution)/shard_map/psum | solution.py:164
  1153.6 3.2 fusion.79
  1156.8 5.2 dynamic-slice_reduce_fusion.2
  1162.1 3.2 multiply_convert_fusion.2
  1165.2 122.8 %all-reduce.11.cloned.1.call-done = (f32[4096]{0:T(1024)}, f32[2048]{0:T(1024)}, f32[8192]{0:T(1024)}, f32[2048]{0:T(1024)}, f32[2048]{0:T(1024)}, /*index=5*/f32[2048]{0:T(1024)}, f32[2048]{0:T(1024)}, f32[2048]{0:T(1024)}) async-done(((f32[4096]{0:T(1024)}, f32[2048]{0:T(1024)}, f32[8192]{0:T(1024)}, f32[2048]{0:T(1024)}, f32[2048]{0:T(1024)}, /*index=5*/f32[2048]{0:T(1024)}, f32[2048]{0:T(1024)}, ...) | async-done | bytes 98320 | tf_op jit(solution)/shard_map/psum | solution.py:295
  (242 shorter events, 97.1 us)
Async XLA Ops:
  7.2 48.4 %all-gather.4.cloned.1.call-start = ((), (), s32[]{:S(2)}) async-start(), calls=%async_computation.4 | async-start | bytes 3932160 | tf_op jit(solution)/shard_map/all_gather | solution.py:75
  9.6 107.9 %all-gather.6.cloned.1.call-start = ((), (), s32[]{:S(2)}) async-start(), calls=%async_computation.5 | async-start | bytes 1310720 | tf_op jit(solution)/shard_map/all_gather | solution.py:76
  11.5 290.1 %all-reduce.7.cloned.1.call-start = ((), (), s32[]{:S(2)}) async-start(), calls=%async_computation.6 | async-start | bytes 16777216 | tf_op jit(solution)/shard_map/psum | solution.py:152
  13.3 6.0 copy-start.3
  13.4 42.2 %copy-start.23 = (f32[2048]{0:T(1024)S(1)}, f32[2048]{0:T(1024)}, u32[]{:S(2)}) copy-start(f32[2048]{0:T(1024)} %param.32) | copy-start | bytes 24580
  13.4 42.2 %copy-start.33 = (f32[2048]{0:T(1024)S(1)}, f32[2048]{0:T(1024)}, u32[]{:S(2)}) copy-start(f32[2048]{0:T(1024)} %param.33) | copy-start | bytes 24580
  19.2 282.3 %copy-start.16 = (f32[2048]{0:T(1024)}, f32[2048]{0:T(1024)S(1)}, u32[]{:S(2)}) copy-start(f32[2048]{0:T(1024)S(1)} %broadcast_multiply_fusion.3) | copy-start | bytes 24580
  21.6 280.0 %copy-start.20 = (f32[2048]{0:T(1024)}, f32[2048]{0:T(1024)S(1)}, u32[]{:S(2)}) copy-start(f32[2048]{0:T(1024)S(1)} %add_rsqrt_fusion.1) | copy-start | bytes 24580
  117.5 8.3 copy-start.1
  117.5 8.3 copy-start.4
  117.5 8.3 copy-start.6
  117.5 8.3 copy-start.11
  125.8 230.8 %all-gather.8.cloned.1.call-start = ((), (), s32[]{:S(2)}) async-start(), calls=%async_computation.7 | async-start | bytes 5242880 | tf_op jit(solution)/shard_map/all_gather | solution.py:77
  125.9 6.8 copy-start.10
  128.4 173.1 %copy-start.26 = (f32[2048]{0:T(1024)S(1)}, f32[2048]{0:T(1024)}, u32[]{:S(2)}) copy-start(f32[2048]{0:T(1024)} %param.27) | copy-start | bytes 24580
  131.4 27.1 %collective-permute-start = (bf16[512,1024]{1,0:T(8,128)(2,1)S(1)}, bf16[512,1024]{1,0:T(8,128)(2,1)}, u32[]{:S(2)}, u32[]{:S(2)}) collective-permute-start(bf16[512,1024]{1,0:T(8,128)(2,1)S(1)} %get-tuple-element.303), channel_id=1, source_target_pairs={{0,8},{8,16},{16,24},{24,0},{1,9},{9,17},{17,25},{25,1},{2,10},{10... | collective-permute-start | bytes 3145736 | tf_op jit(solution)/shard_map/ppermute | solution.py:18
  133.9 446.0 %all-reduce.9.cloned.1.call-start = ((), (), s32[]{:S(2)}) async-start(), calls=%async_computation.8 | async-start | bytes 16777216 | tf_op jit(solution)/shard_map/psum | solution.py:182
  134.0 46.8 %collective-permute-start.1 = (bf16[512,1024]{1,0:T(8,128)(2,1)S(1)}, bf16[512,1024]{1,0:T(8,128)(2,1)S(1)}, u32[]{:S(2)}, u32[]{:S(2)}) collective-permute-start(bf16[512,1024]{1,0:T(8,128)(2,1)S(1)} %get-tuple-element.303), channel_id=1, source_target_pairs={{0,24},{8,0},{16,8},{24,16},{1,25},{9,1},{17,9},{25,17},{2,26},{10... | collective-permute-start | bytes 3145736 | tf_op jit(solution)/shard_map/ppermute | solution.py:23
  158.4 43.7 %collective-permute-start.2 = (bf16[512,1024]{1,0:T(8,128)(2,1)}, bf16[512,1024]{1,0:T(8,128)(2,1)S(1)}, u32[]{:S(2)}, u32[]{:S(2)}) collective-permute-start(bf16[512,1024]{1,0:T(8,128)(2,1)} %collective-permute-done), channel_id=1, source_target_pairs={{0,8},{8,16},{16,24},{24,0},{1,9},{9,17},{17,25},{25,1},{2,10},{10... | collective-permute-start | bytes 3145736 | tf_op jit(solution)/shard_map/ppermute | solution.py:18
  159.6 459.3 %copy-start.27 = (f32[1024]{0:T(1024)}, f32[1024]{0:T(1024)S(1)}, u32[]{:S(2)}) copy-start(f32[1024]{0:T(1024)S(1)} %dynamic_slice.59) | copy-start | bytes 12292
  159.6 459.3 %copy-start.19 = (f32[2048]{0:T(1024)}, f32[2048]{0:T(1024)S(1)}, u32[]{:S(2)}) copy-start(f32[2048]{0:T(1024)S(1)} %compare_convert_fusion) | copy-start | bytes 24580
  326.7 30.0 %copy-start.22 = (f32[2048]{0:T(1024)S(1)}, f32[2048]{0:T(1024)}, u32[]{:S(2)}) copy-start(f32[2048]{0:T(1024)} %param.34) | copy-start | bytes 24580
  326.7 30.0 %copy-start.32 = (f32[2048]{0:T(1024)S(1)}, f32[2048]{0:T(1024)}, u32[]{:S(2)}) copy-start(f32[2048]{0:T(1024)} %param.35) | copy-start | bytes 24580
  369.9 21.4 %copy-start.35 = (f32[2048,1024]{1,0:T(8,128)}, f32[2048,1024]{1,0:T(8,128)S(1)}, u32[]{:S(2)}) copy-start(f32[2048,1024]{1,0:T(8,128)S(1)} %fusion.75) | copy-start | bytes 25165828
  369.9 23.4 %copy-start.30 = (bf16[2048,1024]{1,0:T(8,128)(2,1)S(1)}, bf16[2048,1024]{1,0:T(8,128)(2,1)}, u32[]{:S(2)}) copy-start(bf16[2048,1024]{1,0:T(8,128)(2,1)} %all-gather.8.cloned.1.call-done) | copy-start | bytes 12582916
  391.3 2.0 copy-start.36
  404.2 414.6 %reduce-scatter.7.cloned.1.call-start = ((), (), s32[]{:S(2)}) async-start(), calls=%async_computation.10 | async-start | bytes 1310720 | tf_op jit(solution)/shard_map/reduce_scatter | solution.py:285
  590.4 24.8 %copy-start.8 = (bf16[4,512,2,128]{3,2,1,0:T(2,128)(2,1)S(1)}, bf16[4,512,2,128]{3,2,1,0:T(2,128)(2,1)}, u32[]{:S(2)}) copy-start(bf16[4,512,2,128]{3,2,1,0:T(2,128)(2,1)} %get-tuple-element.126) | copy-start | bytes 3145732
  609.5 5.7 copy-start
  618.8 201.7 %reduce-scatter.11.cloned.1.call-start = ((), (), s32[]{:S(2)}) async-start(), calls=%async_computation.12 | async-start | bytes 5242880 | tf_op jit(solution)/shard_map/reduce_scatter | solution.py:291
  635.8 187.6 %reduce-scatter.9.cloned.1.call-start = ((), (), s32[]{:S(2)}) async-start(), calls=%async_computation.11 | async-start | bytes 5242880 | tf_op jit(solution)/shard_map/reduce_scatter | solution.py:288
  651.2 9.8 copy-start.2
  651.2 9.8 copy-start.12
  651.2 174.9 %reduce-scatter.5.cloned.1.call-start = ((), (), s32[]{:S(2)}) async-start(), calls=%async_computation.9 | async-start | bytes 3932160 | tf_op jit(solution)/shard_map/reduce_scatter | solution.py:282
  664.4 4.3 copy-start.7
  668.7 3.7 copy-start.5
  676.3 2.6 copy-start.13
  680.3 2.4 copy-start.14
  685.9 4.4 copy-start.7
  690.2 5.0 copy-start.5
  699.1 2.6 copy-start.13
  703.0 2.4 copy-start.14
  708.6 4.3 copy-start.7
  712.9 5.0 copy-start.5
  721.8 2.6 copy-start.13
  725.7 2.4 copy-start.14
  731.3 4.3 copy-start.7
  735.6 5.0 copy-start.5
  744.5 2.6 copy-start.13
  748.4 2.4 copy-start.14
  752.2 8.0 copy-start.17
  752.2 8.0 copy-start.21
  752.2 8.0 copy-start.24
  752.2 8.0 copy-start.34
  760.2 13.2 %copy-start.28 = (f32[1024]{0:T(1024)S(1)}, f32[1024]{0:T(1024)}, u32[]{:S(2)}) copy-start(f32[1024]{0:T(1024)} %copy-done.27) | copy-start | bytes 12292
  773.3 17.9 %copy-start.9 = (bf16[2048,2,3,128]{0,3,2,1:T(8,128)(2,1)S(1)}, bf16[2048,2,3,128]{0,3,2,1:T(8,128)(2,1)}, u32[]{:S(2)}) copy-start(bf16[2048,2,3,128]{0,3,2,1:T(8,128)(2,1)} %copy.80) | copy-start | bytes 9437188
  773.3 380.3 %all-reduce.13.cloned.1.call-start = ((), (), s32[]{:S(2)}) async-start(), calls=%async_computation.14 | async-start | bytes 33554432 | tf_op jit(solution)/shard_map/psum | solution.py:164
  773.4 17.8 %copy-start.31 = (bf16[2048,768]{1,0:T(8,128)(2,1)S(1)}, bf16[2048,768]{1,0:T(8,128)(2,1)}, u32[]{:S(2)}) copy-start(bf16[2048,768]{1,0:T(8,128)(2,1)} %all-gather.4.cloned.1.call-done) | copy-start | bytes 9437188
  800.3 0.9 copy-start.29
  800.4 487.7 %all-reduce.11.cloned.1.call-start = ((), (), s32[]{:S(2)}) async-start(), calls=%async_computation.13 | async-start | bytes 196608 | tf_op jit(solution)/shard_map/psum | solution.py:295
  801.8 11.3 copy-start.15
  818.7 343.3 %copy-start.18 = (f32[16,2,128]{2,1,0:T(2,128)}, f32[16,2,128]{2,1,0:T(2,128)S(1)}, u32[]{:S(2)}) copy-start(f32[16,2,128]{2,1,0:T(2,128)S(1)} %constant_dynamic-update-slice_fusion) | copy-start | bytes 49156
  823.3 338.7 %copy-start.25 = (f32[2048]{0:T(1024)S(1)}, f32[2048]{0:T(1024)}, u32[]{:S(2)}) copy-start(f32[2048]{0:T(1024)} %param.31) | copy-start | bytes 24580
Sparse Core Ops, SparseCore 0:
  10.4 45.1 all-gather.3
  58.0 26.6 all-gather.5
  125.9 175.5 all-reduce.6
  303.8 52.8 all-gather.7
  404.3 175.5 all-reduce.8
  619.0 27.8 reduce-scatter.6
  650.1 52.6 reduce-scatter.10
  705.8 52.6 reduce-scatter.8
  773.5 43.8 reduce-scatter.4
  820.0 333.5 all-reduce.12
  1162.3 125.6 all-reduce.10
